TPU v7x, 32 devices: a whole 2x2x4 slice. The times are simulated.
32 devices in a mesh: strike: 8 (over y, x, core), dip: 4 (over z).
Axes of the slice: x: 2, y: 2, z: 4, core: 2. Of those that a mesh axis runs over, the one named last changes fastest.
Arguments:
- slip: float32 [8192, 2048], P('strike', 'dip'), may hold values from -4 to 8
- slip_rate: float32 [8192, 2048], P('strike', 'dip'), may hold values from -6 to 6
- state: float32 [8192, 2048], P('strike', 'dip'), may hold values from -1 to 1
- loading: float32 [8192, 2048], P('strike', 'dip'), may hold values from -8 to 8
- normal_stress: float32 [8192, 2048], P('strike', 'dip'), may hold values from 0.5 to 2
- patch: int32 [8192, 2048], P('strike', 'dip'), may hold values from 0 to 3
- rate_coef: float32 [4], replicated, may hold values from 0.3 to 1
- state_coef: float32 [4], replicated, may hold values from 0.3 to 1
- slip_scale: float32 [4], replicated, may hold values from 0.5 to 2
- kernel: bfloat16 [16, 2048, 8192], P(None, ('strike', 'dip')), may hold values from -1.5 to 1.5
- history: bfloat16 [16, 2, 2048, 8192], P(None, None, ('strike', 'dip')), may hold values from -6 to 6
Outputs:
- new_rate: float32 [8192, 2048], P('strike', 'dip')
- new_state: float32 [8192, 2048], P('strike', 'dip')
- transfer_stress: float32 [8192, 2048], P('strike', 'dip')
- rate_modes: bfloat16 [2, 2048, 8192], P(None, ('strike', 'dip'))
All inputs are finite; a program needn't handle non-finite values.
Results may differ from a plain program's by a relative error of at most 0.001.
Values sent between devices are 32-bit elements; how exact they have to be, the bound alone decides.
A program may use at most 192 MiB of HBM per device.

v0:
```python
import math
import jax
import jax.numpy as jnp
from jax import lax
from jax.sharding import PartitionSpec as P

NEWTON = 8
shear_modulus = 1.0
damping = 0.5
relaxation = 0.35
time_step = 0.1


def inverse_sinh(value):
    size_v = jnp.abs(value)
    square = size_v * size_v
    result = jnp.log1p(size_v + square / (1.0 + jnp.sqrt(square + 1.0)))
    return jnp.where(value < 0.0, -result, result)


def tables(count_in, count_out, modulus, sign):
    row_index = lax.broadcasted_iota(jnp.int32, (count_in, count_out), 0)
    col_index = lax.broadcasted_iota(jnp.int32, (count_in, count_out), 1)
    angles = 2.0 * math.pi / modulus * (row_index * col_index % modulus).astype(jnp.float32)
    return (jnp.cos(angles), sign * jnp.sin(angles))


def cproduct(pattern, part_re, part_im, table_re, table_im):

    def product(left_op, right_op):
        return jnp.einsum(pattern, left_op, right_op, precision=lax.Precision.HIGHEST)

    if part_im is None:
        return (product(part_re, table_re), product(part_re, table_im))
    return (
        product(part_re, table_re) - product(part_im, table_im),
        product(part_re, table_im) + product(part_im, table_re),
    )


def factors(length):
    inner_len = 128
    return (length // inner_len, inner_len)


def transform_rows(part_re, part_im, sign, flipped):
    row_count, length = part_re.shape
    outer_len, inner_len = factors(length)
    part_re = part_re.reshape(row_count, outer_len, inner_len)
    if part_im is not None:
        part_im = part_im.reshape(row_count, outer_len, inner_len)
    first_re, first_im = tables(outer_len, outer_len, outer_len, sign)
    part_re, part_im = cproduct("rab,ac->rcb", part_re, part_im, first_re, first_im)
    twist_re, twist_im = tables(outer_len, inner_len, length, sign)
    part_re, part_im = (
        part_re * twist_re - part_im * twist_im,
        part_re * twist_im + part_im * twist_re,
    )
    second_re, second_im = tables(inner_len, inner_len, inner_len, sign)
    pattern = "rcb,bm->mcr" if flipped else "rcb,bm->rmc"
    part_re, part_im = cproduct(pattern, part_re, part_im, second_re, second_im)
    out_shape = (length, row_count) if flipped else (row_count, length)
    factor = 1.0 / math.sqrt(length)
    return (part_re.reshape(out_shape) * factor, part_im.reshape(out_shape) * factor)


def transform_cols(part_re, part_im, sign):
    length, col_count = part_re.shape
    outer_len, inner_len = factors(length)
    part_re = part_re.reshape(outer_len, inner_len, col_count)
    part_im = part_im.reshape(outer_len, inner_len, col_count)
    first_re, first_im = tables(outer_len, outer_len, outer_len, sign)
    part_re, part_im = cproduct("abr,ac->cbr", part_re, part_im, first_re, first_im)
    twist_re, twist_im = tables(outer_len, inner_len, length, sign)
    twist_re = twist_re[:, :, None]
    twist_im = twist_im[:, :, None]
    part_re, part_im = (
        part_re * twist_re - part_im * twist_im,
        part_re * twist_im + part_im * twist_re,
    )
    second_re, second_im = tables(inner_len, inner_len, inner_len, sign)
    part_re, part_im = cproduct("cbr,bm->rmc", part_re, part_im, second_re, second_im)
    factor = 1.0 / math.sqrt(length)
    return (
        part_re.reshape(col_count, length) * factor,
        part_im.reshape(col_count, length) * factor,
    )


def wavenumber(index, count):
    return 2.0 * math.pi / count * ((index + count // 2) % count - count // 2).astype(jnp.float32)


def lookup(patch, table):
    result = jnp.zeros(patch.shape, jnp.float32)
    for label in range(table.shape[0]):
        result = jnp.where(patch == label, table[label], result)
    return result


def friction(slip_rate, state, loading, normal_stress, transfer, coef_a, coef_b, length_l):
    stress = loading + transfer
    prefix = 2.0 * jnp.exp(-state / coef_a)
    angle_w = inverse_sinh(slip_rate / prefix)
    for iteration in range(NEWTON):
        residue = normal_stress * coef_a * angle_w + damping * prefix * jnp.sinh(angle_w) - stress
        slope = normal_stress * coef_a + damping * prefix * jnp.cosh(angle_w)
        ratio = residue / slope
        angle_w = angle_w - relaxation * ratio / (1.0 + jnp.abs(ratio))
    new_rate = prefix * jnp.sinh(angle_w)
    new_state = state + time_step * (coef_b / length_l) * (
        jnp.exp(-state / coef_b) - jnp.abs(new_rate)
    )
    return (new_rate, new_state)


def per_device(
    slip,
    slip_rate,
    state,
    loading,
    normal_stress,
    patch,
    rate_coef,
    state_coef,
    slip_scale,
    kernel,
    history,
):
    strike_count = lax.axis_size("strike")
    dip_count = lax.axis_size("dip")
    slip_rows, rate_rows = (
        lax.all_to_all(slip, "dip", split_axis=0, concat_axis=1, tiled=True),
        lax.all_to_all(slip_rate, "dip", split_axis=0, concat_axis=1, tiled=True),
    )
    slip_re, slip_im = transform_rows(slip_rows, None, -1.0, True)
    rate_re, rate_im = transform_rows(rate_rows, None, -1.0, True)
    pieces = (
        lax.all_to_all(slip_re, ("strike", "dip"), split_axis=0, concat_axis=1, tiled=True),
        lax.all_to_all(slip_im, ("strike", "dip"), split_axis=0, concat_axis=1, tiled=True),
        lax.all_to_all(rate_re, ("strike", "dip"), split_axis=0, concat_axis=1, tiled=True),
        lax.all_to_all(rate_im, ("strike", "dip"), split_axis=0, concat_axis=1, tiled=True),
    )
    slip_re, slip_im = transform_rows(pieces[0], pieces[1], -1.0, False)
    rate_re, rate_im = transform_rows(pieces[2], pieces[3], -1.0, False)
    band, total_x = slip_re.shape
    total_y = band * strike_count * dip_count
    offset = (lax.axis_index("strike") * dip_count + lax.axis_index("dip")) * band
    wave_y = wavenumber(offset + lax.broadcasted_iota(jnp.int32, (band,), 0), total_y)
    wave_x = wavenumber(lax.broadcasted_iota(jnp.int32, (total_x,), 0), total_x)
    magnitude = jnp.sqrt(wave_y[:, None] ** 2 + wave_x[None, :] ** 2)
    memory_re = jnp.einsum("jrc,jrc->rc", kernel, history[:, 0], preferred_element_type=jnp.float32)
    memory_im = jnp.einsum("jrc,jrc->rc", kernel, history[:, 1], preferred_element_type=jnp.float32)
    static = -0.5 * shear_modulus * magnitude
    stress_re = static * slip_re + memory_re
    stress_im = static * slip_im + memory_im
    rate_modes = jnp.stack([rate_re, rate_im]).astype(jnp.bfloat16)
    back_re, back_im = transform_rows(stress_re, stress_im, 1.0, False)
    back = (
        lax.all_to_all(back_re, ("strike", "dip"), split_axis=1, concat_axis=0, tiled=True),
        lax.all_to_all(back_im, ("strike", "dip"), split_axis=1, concat_axis=0, tiled=True),
    )
    line_re, line_im = transform_cols(back[0], back[1], 1.0)
    transfer = lax.all_to_all(line_re, "dip", split_axis=1, concat_axis=0, tiled=True)
    coef_a = lookup(patch, rate_coef)
    coef_b = lookup(patch, state_coef)
    length_l = lookup(patch, slip_scale)
    new_rate, new_state = friction(
        slip_rate, state, loading, normal_stress, transfer, coef_a, coef_b, length_l
    )
    return (new_rate, new_state, transfer, rate_modes)


def solution(mesh):
    return jax.shard_map(
        per_device,
        mesh=mesh,
        in_specs=(
            P("strike", "dip"),
            P("strike", "dip"),
            P("strike", "dip"),
            P("strike", "dip"),
            P("strike", "dip"),
            P("strike", "dip"),
            P(),
            P(),
            P(),
            P(None, ("strike", "dip"), None),
            P(None, None, ("strike", "dip"), None),
        ),
        out_specs=(
            P("strike", "dip"),
            P("strike", "dip"),
            P("strike", "dip"),
            P(None, ("strike", "dip"), None),
        ),
        check_vma=False,
    )
```

profile of v0, /device:TPU:0, one launch (start us, length us, event | category | flops | bytes accessed | tf_op | source)
XLA Modules:
  0.0 581.7 jit_solution(3470144887140389631)
XLA Ops:
  0.6 54.6 %all_to_all.126 = f32[4,256,512]{2,1,0:T(8,128)S(1)} all-to-all(f32[4,256,512]{2,1,0:T(8,128)} %bitcast.262), channel_id=1, replica_groups=mesh['strike'=8,'dip'=4] {'dip'}, dimensions={0} | all-to-all | bytes 4194304 | tf_op jit(solution)/shard_map/all_to_all | solution.py:134
  55.2 4.5 all-to-all-start
  71.0 36.1 %all-to-all-done = f32[4,256,512]{2,1,0:T(8,128)} async-done(((f32[4,256,512]{2,1,0:T(8,128)}), f32[4,256,512]{2,1,0:T(8,128)}, u32[]{:S(2)}, u32[]{:S(2)}) %all-to-all-start) | async-done | bytes 2097184 | tf_op jit(solution)/shard_map/all_to_all | solution.py:133
  107.1 4.3 copy.130
  116.9 5.5 subtract_bitcast_fusion
  134.5 4.4 fusion.99
  144.2 37.2 %all-to-all-done.2 = f32[32,64,256]{2,1,0:T(8,128)} async-done(((f32[32,64,256]{2,1,0:T(8,128)}), f32[32,64,256]{2,1,0:T(8,128)}, u32[]{:S(2)}, u32[]{:S(2)}) %all-to-all-start.2) | async-done | bytes 2097184 | tf_op jit(solution)/shard_map/all_to_all | solution.py:140
  181.3 4.7 all-to-all-start.1
  186.4 4.2 fusion.83
  195.9 36.8 %all-to-all-done.1 = f32[32,64,256]{2,1,0:T(8,128)} async-done(((f32[32,64,256]{2,1,0:T(8,128)}), f32[32,64,256]{2,1,0:T(8,128)}, u32[]{:S(2)}, u32[]{:S(2)}) %all-to-all-start.1) | async-done | bytes 2097184 | tf_op jit(solution)/shard_map/all_to_all | solution.py:139
  232.7 5.2 all-to-all-start.7
  237.9 20.0 %fusion.1 = (f32[64,8192]{1,0:T(8,128)}, f32[64,8192]{1,0:T(8,128)}) fusion(bf16[16,64,8192]{2,1,0:T(8,128)(2,1)} %param.20, bf16[16,2,64,8192]{3,2,1,0:T(8,128)(2,1)} %param.21), kind=kLoop, calls=%fused_computation.3 | loop fusion | flops 57671680 | bytes 54525952 | tf_op jit(solution)/shard_map/jrc,jrc->rc/dot_general | solution.py:153
  257.9 4.2 fusion.81
  271.7 4.1 copy.136
  287.7 6.3 %all-to-all-start.8 = ((f32[32,64,256]{2,1,0:T(8,128)}), f32[32,64,256]{2,1,0:T(8,128)}, u32[]{:S(2)}, u32[]{:S(2)}) async-start(f32[32,64,256]{2,1,0:T(8,128)} %bitcast.255), calls=%async_computation.8 | async-start | bytes 4194304 | tf_op jit(solution)/shard_map/all_to_all | solution.py:142
  305.3 4.8 mul.985
  321.4 5.3 mul.989
  349.7 4.8 mul.1001
  354.5 4.1 copy.149
  358.7 6.1 %all-to-all-start.4 = ((f32[64,32,256]{2,0,1:T(8,128)}), f32[64,32,256]{2,0,1:T(8,128)}, u32[]{:S(2)}, u32[]{:S(2)}) async-start(f32[64,32,256]{2,0,1:T(8,128)} %copy.149), calls=%async_computation.4 | async-start | bytes 4194304 | tf_op jit(solution)/shard_map/all_to_all | solution.py:161
  382.1 29.6 %all-to-all-done.4 = f32[64,32,256]{2,0,1:T(8,128)} async-done(((f32[64,32,256]{2,0,1:T(8,128)}), f32[64,32,256]{2,0,1:T(8,128)}, u32[]{:S(2)}, u32[]{:S(2)}) %all-to-all-start.4) | async-done | bytes 2097184 | tf_op jit(solution)/shard_map/all_to_all | solution.py:161
  411.7 4.7 all-to-all-start.3
  426.6 4.9 copy.173
  438.8 5.7 fusion.91
  444.5 5.7 fusion.89
  450.2 12.8 %all-to-all-done.3 = f32[64,32,256]{2,0,1:T(8,128)} async-done(((f32[64,32,256]{2,0,1:T(8,128)}), f32[64,32,256]{2,0,1:T(8,128)}, u32[]{:S(2)}, u32[]{:S(2)}) %all-to-all-start.3) | async-done | bytes 2097184 | tf_op jit(solution)/shard_map/all_to_all | solution.py:160
  463.0 5.5 fusion.109
  468.5 5.3 multiply_subtract_fusion.1
  483.0 5.3 all-to-all-start.5
  500.4 4.4 mul.1062
  517.3 20.5 %all-to-all-done.5 = f32[256,4,512]{0,2,1:T(8,128)} async-done(((f32[256,4,512]{0,2,1:T(8,128)}), f32[256,4,512]{0,2,1:T(8,128)}, u32[]{:S(2)}, u32[]{:S(2)}) %all-to-all-start.5) | async-done | bytes 2097184 | tf_op jit(solution)/shard_map/all_to_all | solution.py:164
  540.8 40.4 %multiply_add_fusion.1 = (f32[1024,512]{1,0:T(8,128)}, f32[1024,512]{1,0:T(8,128)}) fusion(f32[1024,512]{1,0:T(8,128)} %param.13, pred[1024,512]{1,0:T(8,128)(4,1)} %get-tuple-element.16, pred[1024,512]{1,0:T(8,128)(4,1)S(1)} %copy-done.22, pred[1024,512]{1,0:T(8,128)(4,1)} %get-tuple-element.17, pred[1024,512]{1,0:T(8,128)(4,1)S(1)} %copy-done.21, ...), kind=kLoop, calls=%fused_computation.102 | loop fusion | flops 120061952 | bytes 16777264 | tf_op jit(solution)/shard_map/add | solution.py:111
  (129 shorter events, 178.0 us)
Async XLA Ops:
  55.2 51.9 %all-to-all-start = ((f32[4,256,512]{2,1,0:T(8,128)}), f32[4,256,512]{2,1,0:T(8,128)}, u32[]{:S(2)}, u32[]{:S(2)}) async-start(f32[4,256,512]{2,1,0:T(8,128)} %bitcast.261), calls=%async_computation | async-start | bytes 4194304 | tf_op jit(solution)/shard_map/all_to_all | solution.py:133
  113.9 2.4 copy-start.15
  113.9 3.0 copy-start.16
  122.5 2.6 copy-start.11
  122.5 2.6 copy-start.6
  130.4 50.9 %all-to-all-start.2 = ((f32[32,64,256]{2,1,0:T(8,128)}), f32[32,64,256]{2,1,0:T(8,128)}, u32[]{:S(2)}, u32[]{:S(2)}) async-start(f32[32,64,256]{2,1,0:T(8,128)} %bitcast.259), calls=%async_computation.2 | async-start | bytes 4194304 | tf_op jit(solution)/shard_map/all_to_all | solution.py:140
  134.5 4.4 copy-start.7
  181.3 51.4 %all-to-all-start.1 = ((f32[32,64,256]{2,1,0:T(8,128)}), f32[32,64,256]{2,1,0:T(8,128)}, u32[]{:S(2)}, u32[]{:S(2)}) async-start(f32[32,64,256]{2,1,0:T(8,128)} %bitcast.256), calls=%async_computation.1 | async-start | bytes 4194304 | tf_op jit(solution)/shard_map/all_to_all | solution.py:139
  232.7 55.0 %all-to-all-start.7 = ((f32[32,64,256]{2,1,0:T(8,128)}), f32[32,64,256]{2,1,0:T(8,128)}, u32[]{:S(2)}, u32[]{:S(2)}) async-start(f32[32,64,256]{2,1,0:T(8,128)} %bitcast.257), calls=%async_computation.7 | async-start | bytes 4194304 | tf_op jit(solution)/shard_map/all_to_all | solution.py:141
  287.7 71.0 %all-to-all-start.8 = ((f32[32,64,256]{2,1,0:T(8,128)}), f32[32,64,256]{2,1,0:T(8,128)}, u32[]{:S(2)}, u32[]{:S(2)}) async-start(f32[32,64,256]{2,1,0:T(8,128)} %bitcast.255), calls=%async_computation.8 | async-start | bytes 4194304 | tf_op jit(solution)/shard_map/all_to_all | solution.py:142
  294.0 3.9 copy-start.4
  310.0 3.9 copy-start.5
  321.4 5.3 copy-start.14
  339.9 2.2 copy-start.2
  358.7 53.0 %all-to-all-start.4 = ((f32[64,32,256]{2,0,1:T(8,128)}), f32[64,32,256]{2,0,1:T(8,128)}, u32[]{:S(2)}, u32[]{:S(2)}) async-start(f32[64,32,256]{2,0,1:T(8,128)} %copy.149), calls=%async_computation.4 | async-start | bytes 4194304 | tf_op jit(solution)/shard_map/all_to_all | solution.py:161
  364.8 3.9 copy-start.3
  382.0 34.6 %copy-start.23 = (f32[4]{0:T(128)S(1)}, f32[4]{0:T(128)}, u32[]{:S(2)}) copy-start(f32[4]{0:T(128)} %param.17) | copy-start | bytes 52
  382.0 35.2 %copy-start.24 = (f32[4]{0:T(128)S(1)}, f32[4]{0:T(128)}, u32[]{:S(2)}) copy-start(f32[4]{0:T(128)} %param.18) | copy-start | bytes 52
  382.0 35.9 %copy-start.25 = (f32[4]{0:T(128)S(1)}, f32[4]{0:T(128)}, u32[]{:S(2)}) copy-start(f32[4]{0:T(128)} %param.19) | copy-start | bytes 52
  382.0 36.6 %copy-start.19 = (s32[1024,512]{1,0:T(8,128)S(1)}, s32[1024,512]{1,0:T(8,128)}, u32[]{:S(2)}) copy-start(s32[1024,512]{1,0:T(8,128)} %param.16) | copy-start | bytes 6291460
  411.7 51.4 %all-to-all-start.3 = ((f32[64,32,256]{2,0,1:T(8,128)}), f32[64,32,256]{2,0,1:T(8,128)}, u32[]{:S(2)}, u32[]{:S(2)}) async-start(f32[64,32,256]{2,0,1:T(8,128)} %copy.146), calls=%async_computation.3 | async-start | bytes 4194304 | tf_op jit(solution)/shard_map/all_to_all | solution.py:160
  426.6 7.9 %copy-start.13 = (f32[64,64,128]{2,1,0:T(8,128)}, f32[64,64,128]{2,1,0:T(8,128)S(1)}, u32[]{:S(2)}) copy-start(f32[64,64,128]{2,1,0:T(8,128)S(1)} %reshape.268) | copy-start | bytes 6291460
  434.5 2.1 copy-start.8
  463.0 5.5 copy-start.17
  483.0 54.7 %all-to-all-start.5 = ((f32[256,4,512]{0,2,1:T(8,128)}), f32[256,4,512]{0,2,1:T(8,128)}, u32[]{:S(2)}, u32[]{:S(2)}) async-start(f32[256,4,512]{0,2,1:T(8,128)} %bitcast.258), calls=%async_computation.5 | async-start | bytes 4194304 | tf_op jit(solution)/shard_map/all_to_all | solution.py:164
  488.3 3.8 copy-start.9
  494.3 2.2 copy-start
  504.8 3.9 copy-start.1
  512.0 2.5 copy-start.18
  537.8 3.0 copy-start.20
  537.8 3.0 copy-start.21
  537.8 3.0 copy-start.22
  (2 other events, 4.1 us)
where the time goes:
time: 590 us; the launch traced here: 582 us
  waiting for transfers between devices  173 us (29%)
  matrix products  136 us (23%)
  local copies, waits for them, and re-layouts  106 us (18%)
  other arithmetic  69.7 us (12%)
  blocking collectives  54.6 us (9%)
  starting transfers between devices  40.7 us (7%)
    dot_general x42, matrix products, product(): jnp.einsum(pattern, left_op, right_op, precision=lax.Precision.HIGHEST)  136 us
    all_to_all x1, blocking collectives, per_device(): lax.all_to_all(slip_rate, 'dip', split_axis=0, concat_axis=1, tiled=True)  54.6 us
    add x1, other arithmetic, friction(): state + time_step * (coef_b / length_l) * (jnp.exp(-state / coef_b) - jnp...  40.4 us
    all_to_all x1, waiting for transfers between devices, per_device(): lax.all_to_all(slip_im, ('strike', 'dip'), split_axis=0, concat_axis=1, t...  37.2 us
    all_to_all x1, waiting for transfers between devices, per_device(): lax.all_to_all(slip_re, ('strike', 'dip'), split_axis=0, concat_axis=1, t...  36.8 us
    all_to_all x1, waiting for transfers between devices, per_device(): lax.all_to_all(slip, 'dip', split_axis=0, concat_axis=1, tiled=True)  36.1 us
    mul x9, local copies, waits for them, and re-layouts, transform_rows(): part_im.reshape(out_shape) * factor  30.7 us
    mul x9, local copies, waits for them, and re-layouts, transform_rows(): part_re.reshape(out_shape) * factor  29.7 us
  transfers between devices with their start and end apart: 8, of which 6 were waited for; matrix products, arithmetic and copies ran while one was open for 39% of the time, Pallas kernels for 0%

commit v1 on v0

--- a/solution.py
+++ b/solution.py
@@ -137,7 +137,15 @@
     rate_re, rate_im = transform_rows(rate_rows, None, -1.0, True)
     pieces = (
         lax.all_to_all(slip_re, ("strike", "dip"), split_axis=0, concat_axis=1, tiled=True),
-        lax.all_to_all(slip_im, ("strike", "dip"), split_axis=0, concat_axis=1, tiled=True),
+        jnp.concatenate(
+            lax.all_to_all(
+                jnp.stack(jnp.split(slip_im, lax.axis_size(("strike", "dip")), axis=0)),
+                ("strike", "dip"),
+                0,
+                0,
+            ),
+            axis=1,
+        ),
         lax.all_to_all(rate_re, ("strike", "dip"), split_axis=0, concat_axis=1, tiled=True),
         lax.all_to_all(rate_im, ("strike", "dip"), split_axis=0, concat_axis=1, tiled=True),
     )

time: 590 us -> 608 us (1.031)
  local copies, waits for them, and re-layouts: 106 us -> 124 us
    unnamed x54 -> x85, local copies, waits for them, and re-layouts: 1.9 us -> 21.5 us
    mul x9 -> x8, local copies, waits for them, and re-layouts: 30.7 us -> 28.2 us  [transform_rows(): part_im.reshape(out_shape) * factor]
  transfers between devices with their start and end apart: 8 -> 8, of which waited for: 6 -> 6; matrix products, arithmetic and copies ran while one was open for 39% -> 37% of each run, Pallas kernels for 0% -> 0%
where the time goes in v1:
time: 608 us; the launch traced here: 601 us
  waiting for transfers between devices  173 us (28%)
  matrix products  136 us (22%)
  local copies, waits for them, and re-layouts  124 us (20%)
  other arithmetic  69.7 us (11%)
  blocking collectives  54.6 us (9%)
  starting transfers between devices  40.7 us (7%)
    dot_general x42, matrix products, product(): jnp.einsum(pattern, left_op, right_op, precision=lax.Precision.HIGHEST)  136 us
    all_to_all x1, blocking collectives, per_device(): lax.all_to_all(slip_rate, 'dip', split_axis=0, concat_axis=1, tiled=True)  54.6 us
    add x1, other arithmetic, friction(): state + time_step * (coef_b / length_l) * (jnp.exp(-state / coef_b) - jnp...  40.4 us
    all_to_all x1, waiting for transfers between devices, per_device(): lax.all_to_all(jnp.stack(jnp.split(slip_im, lax.axis_size(('strike', 'dip...  37.2 us
    all_to_all x1, waiting for transfers between devices, per_device(): lax.all_to_all(slip_re, ('strike', 'dip'), split_axis=0, concat_axis=1, t...  36.8 us
    all_to_all x1, waiting for transfers between devices, per_device(): lax.all_to_all(slip, 'dip', split_axis=0, concat_axis=1, tiled=True)  36.1 us
    mul x9, local copies, waits for them, and re-layouts, transform_rows(): part_re.reshape(out_shape) * factor  29.7 us
    all_to_all x1, waiting for transfers between devices, per_device(): lax.all_to_all(back_im, ('strike', 'dip'), split_axis=1, concat_axis=0, t...  29.6 us
  transfers between devices with their start and end apart: 8, of which 6 were waited for; matrix products, arithmetic and copies ran while one was open for 37% of the time, Pallas kernels for 0%

profile of v1, /device:TPU:0, one launch (start us, length us, event | category | flops | bytes accessed | tf_op | source)
XLA Modules:
  0.0 600.6 jit_solution(8060377563121567887)
XLA Ops:
  0.6 54.6 %all_to_all.118 = f32[4,256,512]{2,1,0:T(8,128)S(1)} all-to-all(f32[4,256,512]{2,1,0:T(8,128)} %bitcast.356), channel_id=1, replica_groups=mesh['strike'=8,'dip'=4] {'dip'}, dimensions={0} | all-to-all | bytes 4194304 | tf_op jit(solution)/shard_map/all_to_all | solution.py:134
  55.2 4.5 all-to-all-start
  71.0 36.1 %all-to-all-done = f32[4,256,512]{2,1,0:T(8,128)} async-done(((f32[4,256,512]{2,1,0:T(8,128)}), f32[4,256,512]{2,1,0:T(8,128)}, u32[]{:S(2)}, u32[]{:S(2)}) %all-to-all-start) | async-done | bytes 2097184 | tf_op jit(solution)/shard_map/all_to_all | solution.py:133
  107.1 4.3 copy.192
  116.9 5.5 subtract_bitcast_fusion
  153.4 4.4 fusion.99
  163.1 37.2 %all-to-all-done.2 = f32[32,64,256]{2,1,0:T(8,128)} async-done(((f32[32,64,256]{2,1,0:T(8,128)}), f32[32,64,256]{2,1,0:T(8,128)}, u32[]{:S(2)}, u32[]{:S(2)}) %all-to-all-start.2) | async-done | bytes 2097184 | tf_op jit(solution)/shard_map/all_to_all | solution.py:141
  200.2 4.7 all-to-all-start.1
  205.3 4.2 fusion.83
  214.8 36.8 %all-to-all-done.1 = f32[32,64,256]{2,1,0:T(8,128)} async-done(((f32[32,64,256]{2,1,0:T(8,128)}), f32[32,64,256]{2,1,0:T(8,128)}, u32[]{:S(2)}, u32[]{:S(2)}) %all-to-all-start.1) | async-done | bytes 2097184 | tf_op jit(solution)/shard_map/all_to_all | solution.py:139
  251.6 5.2 all-to-all-start.7
  256.8 20.0 %fusion.1 = (f32[64,8192]{1,0:T(8,128)}, f32[64,8192]{1,0:T(8,128)}) fusion(bf16[16,64,8192]{2,1,0:T(8,128)(2,1)} %param.20, bf16[16,2,64,8192]{3,2,1,0:T(8,128)(2,1)} %param.21), kind=kLoop, calls=%fused_computation.3 | loop fusion | flops 57671680 | bytes 54525952 | tf_op jit(solution)/shard_map/jrc,jrc->rc/dot_general | solution.py:161
  276.8 4.2 fusion.81
  290.6 4.1 copy.198
  306.6 6.2 %all-to-all-start.8 = ((f32[32,64,256]{2,1,0:T(8,128)}), f32[32,64,256]{2,1,0:T(8,128)}, u32[]{:S(2)}, u32[]{:S(2)}) async-start(f32[32,64,256]{2,1,0:T(8,128)} %bitcast.350), calls=%async_computation.8 | async-start | bytes 4194304 | tf_op jit(solution)/shard_map/all_to_all | solution.py:150
  324.2 4.8 mul.981
  340.3 5.3 mul.985
  368.6 4.8 mul.997
  373.4 4.1 copy.242
  377.6 6.1 %all-to-all-start.4 = ((f32[64,32,256]{2,0,1:T(8,128)}), f32[64,32,256]{2,0,1:T(8,128)}, u32[]{:S(2)}, u32[]{:S(2)}) async-start(f32[64,32,256]{2,0,1:T(8,128)} %copy.242), calls=%async_computation.4 | async-start | bytes 4194304 | tf_op jit(solution)/shard_map/all_to_all | solution.py:169
  400.9 29.6 %all-to-all-done.4 = f32[64,32,256]{2,0,1:T(8,128)} async-done(((f32[64,32,256]{2,0,1:T(8,128)}), f32[64,32,256]{2,0,1:T(8,128)}, u32[]{:S(2)}, u32[]{:S(2)}) %all-to-all-start.4) | async-done | bytes 2097184 | tf_op jit(solution)/shard_map/all_to_all | solution.py:169
  430.6 4.7 all-to-all-start.3
  445.6 4.9 copy.266
  457.7 5.7 fusion.91
  463.4 5.7 fusion.89
  469.2 12.8 %all-to-all-done.3 = f32[64,32,256]{2,0,1:T(8,128)} async-done(((f32[64,32,256]{2,0,1:T(8,128)}), f32[64,32,256]{2,0,1:T(8,128)}, u32[]{:S(2)}, u32[]{:S(2)}) %all-to-all-start.3) | async-done | bytes 2097184 | tf_op jit(solution)/shard_map/all_to_all | solution.py:168
  481.9 5.5 fusion.109
  487.4 5.3 multiply_subtract_fusion.1
  501.9 5.3 all-to-all-start.5
  519.3 4.4 mul.1058
  536.2 20.5 %all-to-all-done.5 = f32[256,4,512]{0,2,1:T(8,128)} async-done(((f32[256,4,512]{0,2,1:T(8,128)}), f32[256,4,512]{0,2,1:T(8,128)}, u32[]{:S(2)}, u32[]{:S(2)}) %all-to-all-start.5) | async-done | bytes 2097184 | tf_op jit(solution)/shard_map/all_to_all | solution.py:172
  559.7 40.4 %multiply_add_fusion.1 = (f32[1024,512]{1,0:T(8,128)}, f32[1024,512]{1,0:T(8,128)}) fusion(f32[1024,512]{1,0:T(8,128)} %param.13, pred[1024,512]{1,0:T(8,128)(4,1)} %get-tuple-element.48, pred[1024,512]{1,0:T(8,128)(4,1)S(1)} %copy-done.22, pred[1024,512]{1,0:T(8,128)(4,1)} %get-tuple-element.49, pred[1024,512]{1,0:T(8,128)(4,1)S(1)} %copy-done.21, ...), kind=kLoop, calls=%fused_computation.102 | loop fusion | flops 120061952 | bytes 16777264 | tf_op jit(solution)/shard_map/add | solution.py:111
  (194 shorter events, 196.7 us)
Async XLA Ops:
  55.2 51.9 %all-to-all-start = ((f32[4,256,512]{2,1,0:T(8,128)}), f32[4,256,512]{2,1,0:T(8,128)}, u32[]{:S(2)}, u32[]{:S(2)}) async-start(f32[4,256,512]{2,1,0:T(8,128)} %bitcast.355), calls=%async_computation | async-start | bytes 4194304 | tf_op jit(solution)/shard_map/all_to_all | solution.py:133
  113.9 2.4 copy-start.15
  114.0 3.0 copy-start.16
  122.5 2.6 copy-start.11
  122.5 2.6 copy-start.6
  149.3 50.9 %all-to-all-start.2 = ((f32[32,64,256]{2,1,0:T(8,128)}), f32[32,64,256]{2,1,0:T(8,128)}, u32[]{:S(2)}, u32[]{:S(2)}) async-start(f32[32,64,256]{2,1,0:T(8,128)} %constant_dynamic-update-slice_fusion), calls=%async_computation.2 | async-start | bytes 4194304 | tf_op jit(solution)/shard_map/all_to_all | solution.py:141
  153.4 4.4 copy-start.7
  200.2 51.4 %all-to-all-start.1 = ((f32[32,64,256]{2,1,0:T(8,128)}), f32[32,64,256]{2,1,0:T(8,128)}, u32[]{:S(2)}, u32[]{:S(2)}) async-start(f32[32,64,256]{2,1,0:T(8,128)} %bitcast.351), calls=%async_computation.1 | async-start | bytes 4194304 | tf_op jit(solution)/shard_map/all_to_all | solution.py:139
  251.6 55.0 %all-to-all-start.7 = ((f32[32,64,256]{2,1,0:T(8,128)}), f32[32,64,256]{2,1,0:T(8,128)}, u32[]{:S(2)}, u32[]{:S(2)}) async-start(f32[32,64,256]{2,1,0:T(8,128)} %bitcast.352), calls=%async_computation.7 | async-start | bytes 4194304 | tf_op jit(solution)/shard_map/all_to_all | solution.py:149
  298.9 2.1 copy-start.10
  306.6 71.0 %all-to-all-start.8 = ((f32[32,64,256]{2,1,0:T(8,128)}), f32[32,64,256]{2,1,0:T(8,128)}, u32[]{:S(2)}, u32[]{:S(2)}) async-start(f32[32,64,256]{2,1,0:T(8,128)} %bitcast.350), calls=%async_computation.8 | async-start | bytes 4194304 | tf_op jit(solution)/shard_map/all_to_all | solution.py:150
  312.8 3.9 copy-start.4
  328.9 3.9 copy-start.5
  340.3 5.3 copy-start.14
  358.8 2.2 copy-start.2
  377.6 53.0 %all-to-all-start.4 = ((f32[64,32,256]{2,0,1:T(8,128)}), f32[64,32,256]{2,0,1:T(8,128)}, u32[]{:S(2)}, u32[]{:S(2)}) async-start(f32[64,32,256]{2,0,1:T(8,128)} %copy.242), calls=%async_computation.4 | async-start | bytes 4194304 | tf_op jit(solution)/shard_map/all_to_all | solution.py:169
  383.7 3.9 copy-start.3
  400.9 34.6 %copy-start.23 = (f32[4]{0:T(128)S(1)}, f32[4]{0:T(128)}, u32[]{:S(2)}) copy-start(f32[4]{0:T(128)} %param.17) | copy-start | bytes 52
  400.9 35.3 %copy-start.24 = (f32[4]{0:T(128)S(1)}, f32[4]{0:T(128)}, u32[]{:S(2)}) copy-start(f32[4]{0:T(128)} %param.18) | copy-start | bytes 52
  400.9 35.9 %copy-start.25 = (f32[4]{0:T(128)S(1)}, f32[4]{0:T(128)}, u32[]{:S(2)}) copy-start(f32[4]{0:T(128)} %param.19) | copy-start | bytes 52
  400.9 36.6 %copy-start.19 = (s32[1024,512]{1,0:T(8,128)S(1)}, s32[1024,512]{1,0:T(8,128)}, u32[]{:S(2)}) copy-start(s32[1024,512]{1,0:T(8,128)} %param.16) | copy-start | bytes 6291460
  430.6 51.4 %all-to-all-start.3 = ((f32[64,32,256]{2,0,1:T(8,128)}), f32[64,32,256]{2,0,1:T(8,128)}, u32[]{:S(2)}, u32[]{:S(2)}) async-start(f32[64,32,256]{2,0,1:T(8,128)} %copy.239), calls=%async_computation.3 | async-start | bytes 4194304 | tf_op jit(solution)/shard_map/all_to_all | solution.py:168
  445.6 7.9 %copy-start.13 = (f32[64,64,128]{2,1,0:T(8,128)}, f32[64,64,128]{2,1,0:T(8,128)S(1)}, u32[]{:S(2)}) copy-start(f32[64,64,128]{2,1,0:T(8,128)S(1)} %reshape.327) | copy-start | bytes 6291460
  481.9 5.5 copy-start.17
  501.9 54.7 %all-to-all-start.5 = ((f32[256,4,512]{0,2,1:T(8,128)}), f32[256,4,512]{0,2,1:T(8,128)}, u32[]{:S(2)}, u32[]{:S(2)}) async-start(f32[256,4,512]{0,2,1:T(8,128)} %bitcast.353), calls=%async_computation.5 | async-start | bytes 4194304 | tf_op jit(solution)/shard_map/all_to_all | solution.py:172
  507.2 3.8 copy-start.9
  513.2 2.2 copy-start
  523.7 3.9 copy-start.1
  530.9 2.5 copy-start.18
  556.7 3.0 copy-start.20
  556.7 3.0 copy-start.21
  556.7 3.0 copy-start.22
  (2 other events, 4.1 us)
